TPU v7x, 128 devices: a whole 4x4x4 slice. The times are simulated.
128 devices in a mesh: group: 8 (over y, core), tile: 16 (over x, z).
Axes of the slice: x: 4, y: 4, z: 4, core: 2. Of those that a mesh axis runs over, the one named last changes fastest.
Arguments:
- embeddings: bfloat16 [49152, 768], P(('group', 'tile')), may hold values from -15 to 15
- clusters: int32 [49152], P(('group', 'tile')), may hold values from 0 to 31, as said below
- cluster_owner: int32 [32], replicated, may hold values from 0 to 7, as said below
Outputs:
- neighbours: bfloat16 [49152, 768], P(('group', 'tile'))
- log_mass: float32 [49152], P(('group', 'tile'))
Inputs may be any that keep to these rules, and one draw needn't show every extreme that they name: Among the 384 rows of one device at most 72 belong to clusters of any one group; in every draw one group has exactly 72 rows on every device. `cluster_owner`: each group owns exactly 4 clusters.
All inputs are finite; a program needn't handle non-finite values.
Results may differ from a plain program's by a relative error of at most 0.034.
Values may be sent and summed in bfloat16 or wider, within the bound.
No kernel may reach another device: no remote copies, remote signals or barrier semaphores. Data moves between devices by JAX's collectives and lax.ppermute only.
A program may use at most 128 MiB of HBM per device.

v0:
```python
import math
import jax
import jax.numpy as jnp
from jax import lax
from jax.sharding import PartitionSpec as P

score_scale = 3.0
penalty = 2.0


def block_scores(queries, query_ids, key_rows, key_ids):
    feature_width = queries.shape[1]
    products = lax.dot_general(
        queries, key_rows, (((1,), (1,)), ((), ())), preferred_element_type=jnp.float32
    )
    differs = (query_ids[:, None] != key_ids[None, :]).astype(jnp.float32)
    return products * (score_scale / math.sqrt(feature_width)) - penalty * differs


def partial_terms(scores, usable, key_rows):
    row_peak = jnp.max(jnp.where(usable, scores, 0.0), axis=1)
    weights = jnp.exp(jnp.where(usable, scores - row_peak[:, None], -jnp.inf))
    row_total = jnp.sum(weights, axis=1)
    weighted = jnp.dot(weights.astype(jnp.bfloat16), key_rows, preferred_element_type=jnp.float32)
    return (row_peak, row_total, weighted)


def combine_terms(former, second):
    row_peak = jnp.maximum(former[0], second[0])
    factor_one = jnp.exp(former[0] - row_peak)
    factor_two = jnp.exp(second[0] - row_peak)
    row_total = former[1] * factor_one + second[1] * factor_two
    weighted = second[2] * factor_two[:, None]
    return (row_peak, row_total, weighted)


def per_device(embeddings, clusters, cluster_owner):
    row_count = embeddings.shape[0]
    feature_width = embeddings.shape[1]
    groups_total = lax.axis_size("group")
    capacity = 3 * row_count // (2 * groups_total)
    slot_count = groups_total * capacity
    cluster_total = cluster_owner.shape[0]
    table_hit = clusters[:, None] == jnp.arange(cluster_total, dtype=jnp.int32)[None, :]
    group_of = jnp.sum(jnp.where(table_hit, cluster_owner[None, :], 0), axis=1)
    same_group = group_of[:, None] == group_of[None, :]
    row_index = jnp.arange(row_count, dtype=jnp.int32)
    earlier = row_index[None, :] < row_index[:, None]
    rank_in = jnp.sum(same_group & earlier, axis=1)
    slot_of = group_of * capacity + rank_in
    slot_index = jnp.arange(slot_count, dtype=jnp.int32)
    placing = slot_index[:, None] == slot_of[None, :]
    outgoing = jnp.dot(
        placing.astype(jnp.bfloat16), embeddings, preferred_element_type=jnp.float32
    ).astype(jnp.bfloat16)
    outgoing_ids = jnp.sum(jnp.where(placing, clusters[None, :] + 1, 0), axis=1) - 1
    arrived, arrived_ids = (
        lax.all_to_all(
            outgoing.reshape(groups_total, capacity, feature_width),
            "group",
            split_axis=0,
            concat_axis=0,
            tiled=True,
        ),
        lax.all_to_all(
            outgoing_ids.reshape(groups_total, capacity),
            "group",
            split_axis=0,
            concat_axis=0,
            tiled=True,
        ),
    )
    queries = arrived.reshape(slot_count, feature_width)
    query_ids = arrived_ids.reshape(slot_count)
    start_state = (
        jnp.zeros((slot_count,), jnp.float32),
        jnp.ones((slot_count,), jnp.float32),
        jnp.zeros((slot_count, feature_width), jnp.float32),
    )
    tile_pos = lax.axis_index("tile")
    query_pos = tile_pos * slot_count + jnp.arange(slot_count, dtype=jnp.int32)
    key_rows = lax.all_gather(queries, "tile", axis=0, tiled=True)
    key_ids = lax.all_gather(query_ids, "tile", axis=0, tiled=True)
    key_pos = jnp.arange(key_rows.shape[0], dtype=jnp.int32)
    scores = block_scores(queries, query_ids, key_rows, key_ids)
    usable = (key_ids[None, :] >= 0) & (key_pos[None, :] != query_pos[:, None])
    partials = combine_terms(start_state, partial_terms(scores, usable, key_rows))
    row_peak, row_total, weighted = partials
    lse_slots = row_peak + jnp.log(row_total)
    neighbour_slots = (weighted / row_total[:, None]).astype(jnp.bfloat16)
    back_rows, back_lse = (
        lax.all_to_all(
            neighbour_slots.reshape(groups_total, capacity, feature_width),
            "group",
            split_axis=0,
            concat_axis=0,
            tiled=True,
        ),
        lax.all_to_all(
            lse_slots.reshape(groups_total, capacity).astype(jnp.bfloat16),
            "group",
            split_axis=0,
            concat_axis=0,
            tiled=True,
        ).astype(jnp.float32),
    )
    flat_rows = back_rows.reshape(slot_count, feature_width)
    neighbours = jnp.take(flat_rows, slot_of, axis=0)
    log_mass = jnp.take(back_lse.reshape(slot_count), slot_of, axis=0).astype(jnp.float32)
    return (neighbours, log_mass)


def solution(mesh):
    placed = (P(("group", "tile"), None), P(("group", "tile")), P())
    return jax.shard_map(
        per_device,
        mesh=mesh,
        in_specs=placed,
        out_specs=(P(("group", "tile"), None), P(("group", "tile"))),
        check_vma=False,
    )
```

profile of v0, /device:TPU:1, one launch (start us, length us, event | category | flops | bytes accessed | tf_op | source)
XLA Modules:
  0.0 218.7 jit_solution(13662327656676615391)
XLA Ops:
  7.2 0.8 select_reduce_fusion.2
  8.3 0.7 multiply_add_fusion
  9.0 0.6 convolution_convert_fusion
  9.6 19.4 %all_to_all.22 = bf16[8,72,768]{2,1,0:T(8,128)(2,1)} all-to-all(bf16[8,72,768]{2,1,0:T(8,128)(2,1)S(1)} %bitcast.12), channel_id=1, replica_groups=mesh['group'=8,'tile'=16] {'group'}, dimensions={0} | all-to-all | bytes 1769472 | tf_op jit(solution)/shard_map/all_to_all | solution.py:58
  29.2 0.7 sub.55
  29.9 4.0 %all-to-all-start = ((s32[8,1,72]{2,1,0:T(1,128)}), s32[8,1,72]{2,1,0:T(1,128)S(1)}, u32[]{:S(2)}, u32[]{:S(2)}) async-start(s32[8,1,72]{2,1,0:T(1,128)} %sub.55), calls=%async_computation | async-start | bytes 8192 | tf_op jit(solution)/shard_map/all_to_all | solution.py:65
  33.9 1.2 dynamic-slice
  35.8 2.6 %all-to-all-done = s32[8,1,72]{2,1,0:T(1,128)S(1)} async-done(((s32[8,1,72]{2,1,0:T(1,128)}), s32[8,1,72]{2,1,0:T(1,128)S(1)}, u32[]{:S(2)}, u32[]{:S(2)}) %all-to-all-start) | async-done | bytes 2336 | tf_op jit(solution)/shard_map/all_to_all | solution.py:65
  38.4 0.5 broadcast.121
  38.9 0.7 reduce.9
  39.7 0.3 dynamic-update-slice
  40.0 63.1 %all-reduce = s32[9216]{0:T(1024)S(1)} all-reduce(s32[9216]{0:T(1024)S(1)} %dynamic-update-slice), channel_id=1, replica_groups=mesh['group'=8,'tile'=16] {'tile'}, use_global_device_ids=true, to_apply=%add | all-reduce | flops 9216 | bytes 73728
  103.1 25.9 %all-gather.2.cloned.1.call-done = bf16[9216,768]{1,0:T(8,128)(2,1)} async-done(((bf16[576,768]{1,0:T(8,128)(2,1)}), bf16[9216,768]{1,0:T(8,128)(2,1)}) %all-gather.2.cloned.1.call-update) | async-done | bytes 14155792 | tf_op jit(solution)/shard_map/all_gather | solution.py:82
  128.9 18.6 %select_reduce_fusion = (f32[576]{0:T(1024)S(1)}, f32[576,9216]{1,0:T(8,128)}) fusion(s32[9216]{0:T(1024)S(1)} %all-reduce, s32[576]{0:T(1024)S(1)} %iota_add_fusion, s32[576]{0:T(1024)S(1)} %reshape.184, pred[9216]{0:T(1024)(128)(4,1)S(1)} %broadcast_compare_fusion, bf16[576,768]{1,0:T(8,128)(2,1)} %bitcast.11, ...), kind=kOutput, calls=%fused_computation.3 | convolution fusion | flops 8196193792 | bytes 36327168 | tf_op jit(solution)/shard_map/dot_general | solution.py:13
  147.6 13.3 %fusion.17 = f32[576]{0:T(1024)S(1)} fusion(f32[576]{0:T(1024)S(1)} %get-tuple-element.6, s32[9216]{0:T(1024)S(1)} %all-reduce, s32[576]{0:T(1024)S(1)} %reshape.184, f32[576,9216]{1,0:T(8,128)} %get-tuple-element.7, s32[576]{0:T(1024)S(1)} %iota_add_fusion, pred[9216]{0:T(1024)(128)(4,1)S(1)} %broadcast_compare_fusion), kind=kLoop, calls=%fused_computation.46 | loop fusion | flops 47775168 | bytes 21288960 | tf_op jit(solution)/shard_map/reduce_sum | solution.py:23
  161.0 0.6 copy.5
  161.6 5.0 %all-to-all-start.3 = ((bf16[8,1,72]{2,1,0:T(2,128)(2,1)}), bf16[8,1,72]{2,1,0:T(2,128)(2,1)S(1)}, u32[]{:S(2)}, u32[]{:S(2)}) async-start(bf16[8,1,72]{2,1,0:T(2,128)(2,1)} %copy.5), calls=%async_computation.3 | async-start | bytes 8192 | tf_op jit(solution)/shard_map/all_to_all | solution.py:99
  166.6 24.0 %divide_convert_fusion = bf16[576,768]{1,0:T(8,128)(2,1)} fusion(bf16[9216,768]{1,0:T(8,128)(2,1)} %all-gather.2.cloned.1.call-done, f32[576]{0:T(1024)S(1)} %get-tuple-element.5, f32[576]{0:T(1024)S(1)} %get-tuple-element.4, f32[576,9216]{1,0:T(8,128)} %get-tuple-element.7, f32[576]{0:T(1024)S(1)} %get-tuple-element.6, s32[9216]{0:T(1024)S(1)} %all-reduce, ...), kind=kOutput, calls=%fused_computation.9 | convolution fusion | flops 8202829824 | bytes 36331776 | tf_op jit(solution)/shard_map/dot_general | solution.py:24
  190.6 4.8 %all-to-all-start.2 = ((bf16[8,72,768]{2,1,0:T(8,128)(2,1)}), bf16[8,72,768]{2,1,0:T(8,128)(2,1)S(1)}, u32[]{:S(2)}, u32[]{:S(2)}) async-start(bf16[8,72,768]{2,1,0:T(8,128)(2,1)} %bitcast.3), calls=%async_computation.2 | async-start | bytes 1769472 | tf_op jit(solution)/shard_map/all_to_all | solution.py:92
  195.5 1.9 gather_fusion.1
  197.4 0.6 broadcast_select_fusion.1
  198.0 10.7 %all-to-all-done.2 = bf16[8,72,768]{2,1,0:T(8,128)(2,1)S(1)} async-done(((bf16[8,72,768]{2,1,0:T(8,128)(2,1)}), bf16[8,72,768]{2,1,0:T(8,128)(2,1)S(1)}, u32[]{:S(2)}, u32[]{:S(2)}) %all-to-all-start.2) | async-done | bytes 884768 | tf_op jit(solution)/shard_map/all_to_all | solution.py:92
  208.8 2.2 gather_fusion
  210.9 0.9 broadcast_select_fusion
  (20 shorter events, 0.9 us)
Async XLA Ops:
  7.2 1.8 copy-start
  7.2 121.8 %all-gather.2.cloned.1.call-start = ((), (), s32[]{:S(2)}) async-start(), calls=%async_computation.4 | async-start | bytes 15040512 | tf_op jit(solution)/shard_map/all_gather | solution.py:82
  29.9 8.6 %all-to-all-start = ((s32[8,1,72]{2,1,0:T(1,128)}), s32[8,1,72]{2,1,0:T(1,128)S(1)}, u32[]{:S(2)}, u32[]{:S(2)}) async-start(s32[8,1,72]{2,1,0:T(1,128)} %sub.55), calls=%async_computation | async-start | bytes 8192 | tf_op jit(solution)/shard_map/all_to_all | solution.py:65
  161.6 29.0 %all-to-all-start.3 = ((bf16[8,1,72]{2,1,0:T(2,128)(2,1)}), bf16[8,1,72]{2,1,0:T(2,128)(2,1)S(1)}, u32[]{:S(2)}, u32[]{:S(2)}) async-start(bf16[8,1,72]{2,1,0:T(2,128)(2,1)} %copy.5), calls=%async_computation.3 | async-start | bytes 8192 | tf_op jit(solution)/shard_map/all_to_all | solution.py:99
  190.6 18.1 %all-to-all-start.2 = ((bf16[8,72,768]{2,1,0:T(8,128)(2,1)}), bf16[8,72,768]{2,1,0:T(8,128)(2,1)S(1)}, u32[]{:S(2)}, u32[]{:S(2)}) async-start(bf16[8,72,768]{2,1,0:T(8,128)(2,1)} %bitcast.3), calls=%async_computation.2 | async-start | bytes 1769472 | tf_op jit(solution)/shard_map/all_to_all | solution.py:92
Sparse Core Ops, SparseCore 0:
  29.1 99.7 all-gather.1
where the time goes:
time: 219 us
  blocking collectives  82.4 us (38%)
  matrix products  43.2 us (20%)
  waiting for transfers between devices  39.3 us (18%)
  other arithmetic  17.5 us (8%)
  between operations  14.8 us (7%)
  starting transfers between devices  13.8 us (6%)
  local copies, waits for them, and re-layouts  7.68 us (4%)
    unnamed x1, blocking collectives  63.1 us
    all_gather x1, waiting for transfers between devices, per_device(): key_rows = lax.all_gather(queries, 'tile', axis=0, tiled=True)  25.9 us
    dot_general x1, matrix products, partial_terms(): jnp.dot(weights.astype(jnp.bfloat16), key_rows, preferred_element_type=jn...  24 us
    all_to_all x1, blocking collectives, per_device(): lax.all_to_all(outgoing.reshape(groups_total, capacity, feature_width), '...  19.4 us
    dot_general x1, matrix products, block_scores(): lax.dot_general(queries, key_rows, (((1,), (1,)), ((), ())), preferred_el...  18.6 us
    reduce_sum x1, other arithmetic, partial_terms(): row_total = jnp.sum(weights, axis=1)  13.3 us
    all_to_all x1, waiting for transfers between devices, per_device(): lax.all_to_all(neighbour_slots.reshape(groups_total, capacity, feature_wi...  10.7 us
    all_to_all x1, starting transfers between devices, per_device(): lax.all_to_all(lse_slots.reshape(groups_total, capacity).astype(jnp.bfloa...  4.97 us
  transfers between devices with their start and end apart: 4, of which 3 were waited for; matrix products, arithmetic and copies ran while one was open for 14% of the time, Pallas kernels for 0%

commit v1 on v0

--- a/solution.py
+++ b/solution.py
@@ -79,7 +79,9 @@
     )
     tile_pos = lax.axis_index("tile")
     query_pos = tile_pos * slot_count + jnp.arange(slot_count, dtype=jnp.int32)
-    key_rows = lax.all_gather(queries, "tile", axis=0, tiled=True)
+    key_rows = jnp.concatenate(
+        lax.all_to_all(jnp.stack([queries] * lax.axis_size("tile")), "tile", 0, 0), axis=0
+    )
     key_ids = lax.all_gather(query_ids, "tile", axis=0, tiled=True)
     key_pos = jnp.arange(key_rows.shape[0], dtype=jnp.int32)
     scores = block_scores(queries, query_ids, key_rows, key_ids)

time: 219 us -> 425 us (1.94)
  blocking collectives: 82.4 us -> 295 us
  starting transfers between devices: 13.8 us -> 39.1 us
  waiting for transfers between devices: 39.3 us -> 14.6 us
  between operations: 14.8 us -> 1.41 us
  local copies, waits for them, and re-layouts: 7.68 us -> 13.5 us
    unnamed x1, blocking collectives: 63.1 us -> 278 us
    all_gather x1 -> x0, waiting for transfers between devices: 25.9 us -> none  [per_device(): key_rows = lax.all_gather(queries, 'tile', axis=0, tiled=True)]
    all_to_all x1, starting transfers between devices: 4.97 us -> 20.6 us  [per_device(): lax.all_to_all(lse_slots.reshape(groups_total, capacity).astype(jnp.bfloa...]
    all_to_all x0 -> x1, starting transfers between devices: none -> 7.64 us  [per_device(): lax.all_to_all(jnp.stack([queries] * lax.axis_size('tile')), 'tile', 0, 0)]
    another operation x0 -> x1, local copies, waits for them, and re-layouts: none -> 6.42 us  [per_device(): jnp.stack([queries] * lax.axis_size('tile'))]
  transfers between devices with their start and end apart: 4 -> 4, of which waited for: 3 -> 2; matrix products, arithmetic and copies ran while one was open for 14% -> 7% of each run, Pallas kernels for 0% -> 0%
where the time goes in v1:
time: 425 us; the launch traced here: 424 us
  blocking collectives  295 us (69%)
  matrix products  43 us (10%)
  starting transfers between devices  39.1 us (9%)
  other arithmetic  17.5 us (4%)
  waiting for transfers between devices  14.6 us (3%)
  local copies, waits for them, and re-layouts  13.5 us (3%)
    unnamed x1, blocking collectives  278 us
    dot_general x1, matrix products, partial_terms(): jnp.dot(weights.astype(jnp.bfloat16), key_rows, preferred_element_type=jn...  24 us
    all_to_all x1, starting transfers between devices, per_device(): lax.all_to_all(lse_slots.reshape(groups_total, capacity).astype(jnp.bfloa...  20.6 us
    dot_general x1, matrix products, block_scores(): lax.dot_general(queries, key_rows, (((1,), (1,)), ((), ())), preferred_el...  18.4 us
    all_to_all x1, blocking collectives, per_device(): lax.all_to_all(outgoing.reshape(groups_total, capacity, feature_width), '...  16.6 us
    reduce_sum x1, other arithmetic, partial_terms(): row_total = jnp.sum(weights, axis=1)  13.3 us
    all_to_all x1, waiting for transfers between devices, per_device(): lax.all_to_all(neighbour_slots.reshape(groups_total, capacity, feature_wi...  10.7 us
  transfers between devices with their start and end apart: 4, of which 2 were waited for; matrix products, arithmetic and copies ran while one was open for 7% of the time, Pallas kernels for 0%

profile of v1, /device:TPU:1, one launch (start us, length us, event | category | flops | bytes accessed | tf_op | source)
XLA Modules:
  0.0 424.0 jit_solution(2864152347406307552)
XLA Ops:
  0.6 0.8 select_reduce_fusion.2
  1.7 0.7 multiply_add_fusion
  2.6 0.7 sub.55
  3.3 6.0 %all-to-all-start = ((s32[8,1,72]{2,1,0:T(1,128)}), s32[8,1,72]{2,1,0:T(1,128)S(1)}, u32[]{:S(2)}, u32[]{:S(2)}) async-start(s32[8,1,72]{2,1,0:T(1,128)} %sub.55), calls=%async_computation | async-start | bytes 8192 | tf_op jit(solution)/shard_map/all_to_all | solution.py:65
  9.3 0.6 convolution_convert_fusion
  9.9 3.9 all-to-all-done
  13.8 16.6 %all_to_all.27 = bf16[8,72,768]{2,1,0:T(8,128)(2,1)S(1)} all-to-all(bf16[8,72,768]{2,1,0:T(8,128)(2,1)S(1)} %bitcast.13), channel_id=1, replica_groups=mesh['group'=8,'tile'=16] {'group'}, dimensions={0} | all-to-all | bytes 1769472 | tf_op jit(solution)/shard_map/all_to_all | solution.py:58
  30.3 6.4 %stack.3 = bf16[16,576,768]{2,1,0:T(8,128)(2,1)} broadcast(bf16[576,768]{1,0:T(8,128)(2,1)S(1)} %bitcast.11), dimensions={1,2} | broadcast | bytes 15040512 | tf_op jit(solution)/shard_map/stack | solution.py:83
  36.7 7.6 %all-to-all-start.2 = ((bf16[16,576,768]{2,1,0:T(8,128)(2,1)}), bf16[16,576,768]{2,1,0:T(8,128)(2,1)}, u32[]{:S(2)}, u32[]{:S(2)}) async-start(bf16[16,576,768]{2,1,0:T(8,128)(2,1)} %stack.3), calls=%async_computation.2 | async-start | bytes 28311552 | tf_op jit(solution)/shard_map/all_to_all | solution.py:83
  44.4 0.6 dynamic-slice
  45.7 0.5 broadcast.122
  46.2 0.7 reduce.9
  47.2 278.4 %all-reduce = s32[9216]{0:T(1024)S(1)} all-reduce(s32[9216]{0:T(1024)S(1)} %dynamic-update-slice), channel_id=1, replica_groups=mesh['group'=8,'tile'=16] {'tile'}, use_global_device_ids=true, to_apply=%add | all-reduce | flops 9216 | bytes 73728
  325.7 18.4 %select_reduce_fusion = (f32[576]{0:T(1024)S(1)}, f32[576,9216]{1,0:T(8,128)}) fusion(s32[9216]{0:T(1024)S(1)} %all-reduce, s32[576]{0:T(1024)S(1)} %iota_add_fusion, s32[576]{0:T(1024)S(1)} %reshape.190, pred[9216]{0:T(1024)(128)(4,1)S(1)} %broadcast_compare_fusion, bf16[576,768]{1,0:T(8,128)(2,1)S(1)} %bitcast.12, bf16[9216,768]{1,0:T(8,128)(2,1)} %bitcast.3), kind=kOutput, calls=%fused_computation.3 | convolution fusion | flops 8196193792 | bytes 36327168 | tf_op jit(solution)/shard_map/dot_general | solution.py:13
  344.1 13.3 %fusion.17 = f32[576]{0:T(1024)S(1)} fusion(f32[576]{0:T(1024)S(1)} %get-tuple-element.6, s32[9216]{0:T(1024)S(1)} %all-reduce, s32[576]{0:T(1024)S(1)} %reshape.190, f32[576,9216]{1,0:T(8,128)} %get-tuple-element.7, s32[576]{0:T(1024)S(1)} %iota_add_fusion, pred[9216]{0:T(1024)(128)(4,1)S(1)} %broadcast_compare_fusion), kind=kLoop, calls=%fused_computation.46 | loop fusion | flops 47775168 | bytes 21288960 | tf_op jit(solution)/shard_map/reduce_sum | solution.py:23
  357.5 0.6 copy.5
  358.2 20.6 %all-to-all-start.4 = ((bf16[8,1,72]{2,1,0:T(2,128)(2,1)}), bf16[8,1,72]{2,1,0:T(2,128)(2,1)S(1)}, u32[]{:S(2)}, u32[]{:S(2)}) async-start(bf16[8,1,72]{2,1,0:T(2,128)(2,1)} %copy.5), calls=%async_computation.4 | async-start | bytes 8192 | tf_op jit(solution)/shard_map/all_to_all | solution.py:101
  378.8 24.0 %divide_convert_fusion = bf16[576,768]{1,0:T(8,128)(2,1)} fusion(bf16[9216,768]{1,0:T(8,128)(2,1)} %bitcast.3, f32[576]{0:T(1024)S(1)} %get-tuple-element.5, f32[576]{0:T(1024)S(1)} %get-tuple-element.4, f32[576,9216]{1,0:T(8,128)} %get-tuple-element.7, f32[576]{0:T(1024)S(1)} %get-tuple-element.6, s32[9216]{0:T(1024)S(1)} %all-reduce, ...), kind=kOutput, calls=%fused_computation.9 | convolution fusion | flops 8202829824 | bytes 36331776 | tf_op jit(solution)/shard_map/dot_general | solution.py:24
  402.7 4.8 %all-to-all-start.3 = ((bf16[8,72,768]{2,1,0:T(8,128)(2,1)}), bf16[8,72,768]{2,1,0:T(8,128)(2,1)S(1)}, u32[]{:S(2)}, u32[]{:S(2)}) async-start(bf16[8,72,768]{2,1,0:T(8,128)(2,1)} %bitcast.4), calls=%async_computation.3 | async-start | bytes 1769472 | tf_op jit(solution)/shard_map/all_to_all | solution.py:94
  407.7 1.9 gather_fusion.1
  409.6 0.6 broadcast_select_fusion.1
  410.2 10.7 %all-to-all-done.3 = bf16[8,72,768]{2,1,0:T(8,128)(2,1)S(1)} async-done(((bf16[8,72,768]{2,1,0:T(8,128)(2,1)}), bf16[8,72,768]{2,1,0:T(8,128)(2,1)S(1)}, u32[]{:S(2)}, u32[]{:S(2)}) %all-to-all-start.3) | async-done | bytes 884768 | tf_op jit(solution)/shard_map/all_to_all | solution.py:94
  420.9 2.2 gather_fusion
  423.1 0.9 broadcast_select_fusion
  (22 shorter events, 1.1 us)
Async XLA Ops:
  0.6 8.6 %copy-start = (bf16[384,768]{1,0:T(8,128)(2,1)S(1)}, bf16[384,768]{1,0:T(8,128)(2,1)}, u32[]{:S(2)}) copy-start(bf16[384,768]{1,0:T(8,128)(2,1)} %param.3) | copy-start | bytes 1769476
  3.3 10.5 %all-to-all-start = ((s32[8,1,72]{2,1,0:T(1,128)}), s32[8,1,72]{2,1,0:T(1,128)S(1)}, u32[]{:S(2)}, u32[]{:S(2)}) async-start(s32[8,1,72]{2,1,0:T(1,128)} %sub.55), calls=%async_computation | async-start | bytes 8192 | tf_op jit(solution)/shard_map/all_to_all | solution.py:65
  30.3 14.1 %copy-start.1 = (u32[128]{0:T(128)S(1)}, u32[128]{0:T(128)}, u32[]{:S(2)}) copy-start(u32[128]{0:T(128)} %constant.55) | copy-start | bytes 1540
  36.7 288.9 %all-to-all-start.2 = ((bf16[16,576,768]{2,1,0:T(8,128)(2,1)}), bf16[16,576,768]{2,1,0:T(8,128)(2,1)}, u32[]{:S(2)}, u32[]{:S(2)}) async-start(bf16[16,576,768]{2,1,0:T(8,128)(2,1)} %stack.3), calls=%async_computation.2 | async-start | bytes 28311552 | tf_op jit(solution)/shard_map/all_to_all | solution.py:83
  358.2 44.6 %all-to-all-start.4 = ((bf16[8,1,72]{2,1,0:T(2,128)(2,1)}), bf16[8,1,72]{2,1,0:T(2,128)(2,1)S(1)}, u32[]{:S(2)}, u32[]{:S(2)}) async-start(bf16[8,1,72]{2,1,0:T(2,128)(2,1)} %copy.5), calls=%async_computation.4 | async-start | bytes 8192 | tf_op jit(solution)/shard_map/all_to_all | solution.py:101
  402.7 18.2 %all-to-all-start.3 = ((bf16[8,72,768]{2,1,0:T(8,128)(2,1)}), bf16[8,72,768]{2,1,0:T(8,128)(2,1)S(1)}, u32[]{:S(2)}, u32[]{:S(2)}) async-start(bf16[8,72,768]{2,1,0:T(8,128)(2,1)} %bitcast.4), calls=%async_computation.3 | async-start | bytes 1769472 | tf_op jit(solution)/shard_map/all_to_all | solution.py:94
